TPU v7x, 32 devices: a whole 2x2x4 slice. The times are simulated.
32 devices in a mesh: groups: 2 (over x), ctx: 16 (over z, y, core).
Axes of the slice: x: 2, y: 2, z: 4, core: 2. Of those that a mesh axis runs over, the one named last changes fastest.
Arguments:
- queries: bfloat16 [8192, 4096], P(('groups', 'ctx')), parts along dimension 0, may hold values from -160 to 160
- keys: bfloat16 [8192, 512], P(('groups', 'ctx')), parts along dimension 0, may hold values from -6 to 6
- values: bfloat16 [8192, 512], P(('groups', 'ctx')), parts along dimension 0, may hold values from -6 to 6
- doc_flags: int32 [64], P(('groups', 'ctx')), parts along dimension 0, may hold values from 0 to 1, as said below
Outputs:
- attention: bfloat16 [8192, 4096], P(('groups', 'ctx')), parts along dimension 0
There are 2 independent parts, one for each index of `groups`. A program takes and returns all parts, laid end to end along the dimension named above; each array names one. Nothing has to cross between parts.
Inputs may be any that keep to these rules, and one draw needn't show every extreme that they name: `doc_flags`: block 0 starts a document; every document spans 1 to 6 blocks and one spans exactly 6 blocks.
All inputs are finite; a program needn't handle non-finite values.
Results may differ from a plain program's by a relative error of at most 0.0039.
Values may be sent and summed in bfloat16 or wider, within the bound.
A program may use at most 64 MiB of HBM per device.

v0:
```python
import jax
import jax.numpy as jnp
from jax import lax
from jax.sharding import PartitionSpec as P

HD = 128
KVH = 4
GROUP = 8
BLK = 128
ROUNDS = 4


NEG_FILL = -1e30


def carried_in(value, axis, join, neutral):
    count, mine = (lax.axis_size(axis), lax.axis_index(axis))
    pieces = lax.all_gather(value, axis)
    running = jnp.full_like(value, 0) + jnp.asarray(neutral, value.dtype)

    def lap(position, running):
        longer = join(running, pieces[position])
        return jnp.where(position < mine, longer, running)

    return lax.fori_loop(0, count - 1, lap, running)


def passed_along(value, axis, steps):
    count = lax.axis_size(axis)
    leading, last = (max(0, -steps), min(count, count - steps))
    return lax.ppermute(value, axis, [(source, source + steps) for source in range(leading, last)])


def add_counts(earlier, later):
    return earlier + later


def score_round(q_group, k_round, allowed):
    scored = jnp.einsum("sjd,td->jst", q_group, k_round, preferred_element_type=jnp.float32) * (
        1.0 / HD**0.5
    )
    return jnp.where(allowed[None], scored, NEG_FILL)


def mix_round(rounded, v_round):
    return jnp.einsum("jst,td->sjd", rounded, v_round, preferred_element_type=jnp.float32)


def per_device(queries, keys, values, doc_flags):
    rows = queries.shape[0]
    counted = jnp.sum(doc_flags).reshape(1)
    before = carried_in(counted, "ctx", add_counts, jnp.zeros((1,), jnp.int32))
    labels = (before + jnp.cumsum(doc_flags)).astype(jnp.int32)
    window = [(keys, values, labels)]
    latest = (keys, values, labels)
    for back in range(1, ROUNDS):
        latest = passed_along((latest[0], latest[1], latest[2]), "ctx", 1)
        window.append(latest)
    round_ids = [entry[2] for entry in window]
    place = lax.axis_index("ctx")
    spots = jnp.arange(rows, dtype=jnp.int32)
    query_doc = jnp.repeat(round_ids[0], BLK, total_repeat_length=rows)
    masks = []
    for back in range(ROUNDS):
        key_doc = jnp.repeat(round_ids[back], BLK, total_repeat_length=rows)
        same = query_doc[:, None] == key_doc[None, :]
        if back == 0:
            same = same & (spots[None, :] <= spots[:, None])
        masks.append(same & (place >= back))
    pieces = []
    for group in range(KVH):
        q_group = queries[:, group * GROUP * HD : (group + 1) * GROUP * HD].reshape(rows, GROUP, HD)
        scored = []
        for back in range(ROUNDS):
            k_round = window[back][0][:, group * HD : (group + 1) * HD]
            scored.append(score_round(q_group, k_round, masks[back]))
        top = jnp.max(scored[0], axis=2)
        for back in range(1, ROUNDS):
            top = jnp.maximum(top, jnp.max(scored[back], axis=2))
        total = jnp.zeros(top.shape, jnp.float32)
        mixed = jnp.zeros((rows, GROUP, HD), jnp.float32)
        for back in range(ROUNDS):
            v_round = window[back][1][:, group * HD : (group + 1) * HD]
            weights = jnp.exp(scored[back] - top[:, :, None])
            total = total + jnp.sum(weights, axis=2)
            rounded = weights.astype(jnp.bfloat16)
            mixed = mixed + mix_round(rounded, v_round)
        pieces.append((mixed / total.T[:, :, None]).astype(jnp.bfloat16).reshape(rows, GROUP * HD))
    return jnp.concatenate(pieces, axis=1)


def solution(mesh):
    return jax.shard_map(
        per_device,
        mesh=mesh,
        in_specs=(
            P(("groups", "ctx"), None),
            P(("groups", "ctx"), None),
            P(("groups", "ctx"), None),
            P(("groups", "ctx")),
        ),
        out_specs=P(("groups", "ctx"), None),
        check_vma=False,
    )
```

profile of v0, /device:TPU:0, one launch (start us, length us, event | category | flops | bytes accessed | tf_op | source)
XLA Modules:
  0.0 142.8 jit_solution(3536803541279808419)
XLA Ops:
  4.0 13.7 %all-reduce = s32[16]{0:T(128)S(1)} all-reduce(s32[16]{0:T(128)S(1)} %dynamic-update-slice.7), channel_id=1, replica_groups=mesh['groups'=2,'ctx'=16] {'ctx'}, use_global_device_ids=true, to_apply=%add | all-reduce | flops 16 | bytes 128
  17.7 20.7 %while.18 = (s32[]{:T(128)}, s32[1]{0:T(128)}, s32[]{:T(128)}, s32[16,1]{0,1:T(1,128)S(1)}, s32[]{:T(128)}) while((s32[]{:T(128)}, s32[1]{0:T(128)}, s32[]{:T(128)}, s32[16,1]{0,1:T(1,128)S(1)}, s32[]{:T(128)}) %tuple.88), condition=%wide.region_2.3_spmd, body=%wide.region_1.2_spmd.sunk | while | flops 5 | bytes 107 | solution.py:25
  40.5 4.2 %collective-permute-start.1 = (bf16[256,512]{1,0:T(8,128)(2,1)}, bf16[256,512]{1,0:T(8,128)(2,1)}, u32[]{:S(2)}, u32[]{:S(2)}) collective-permute-start(bf16[256,512]{1,0:T(8,128)(2,1)} %param.19), channel_id=1, source_target_pairs={{0,1},{1,2},{2,3},{3,4},{4,5},{5,6},{6,7},{7,8},{8,9},{9,10},{10,1... | collective-permute-start | bytes 786440 | tf_op jit(solution)/shard_map/ppermute | solution.py:31
  45.8 2.0 %collective-permute-start.6 = (bf16[256,512]{0,1:T(8,128)(2,1)S(1)}, bf16[256,512]{0,1:T(8,128)(2,1)}, u32[]{:S(2)}, u32[]{:S(2)}) collective-permute-start(bf16[256,512]{0,1:T(8,128)(2,1)S(1)} %copy.35), channel_id=1, source_target_pairs={{0,1},{1,2},{2,3},{3,4},{4,5},{5,6},{6,7},{7,8},{8,9},{9,10},{10,1... | collective-permute-start | bytes 786440 | tf_op jit(solution)/shard_map/ppermute | solution.py:31
  48.4 1.8 %fusion.90 = (bf16[256,1024]{1,0:T(8,128)(2,1)S(1)}, bf16[256,1024]{1,0:T(8,128)(2,1)S(1)}, bf16[256,1024]{1,0:T(8,128)(2,1)S(1)}, bf16[256,1024]{1,0:T(8,128)(2,1)S(1)}) fusion(bf16[256,4096]{1,0:T(8,128)(2,1)} %param.18), kind=kLoop, calls=%fused_computation.168 | loop fusion | bytes 4194304 | tf_op jit(solution)/shard_map/slice | solution.py:72
  51.7 2.5 %select_select_fusion.2 = (s32[256]{0:T(256)S(1)}, s32[256]{0:T(256)S(1)}) fusion(s32[]{:T(128)} %bitcast.15, s32[]{:T(128)} %bitcast.14, s32[]{:T(128)} %bitcast.10, s32[]{:T(128)} %bitcast.9), kind=kLoop, calls=%fused_computation.164 | loop fusion | flops 3328 | bytes 2064 | tf_op jit(solution)/shard_map/jit(_take)/select_n | solution.py:65
  54.2 2.3 %collective-permute-start.2 = (s32[2]{0:T(128)S(1)}, s32[2]{0:T(128)S(1)}, u32[]{:S(2)}, u32[]{:S(2)}) collective-permute-start(s32[2]{0:T(128)S(1)} %collective-permute-done), channel_id=1, source_target_pairs={{0,1},{1,2},{2,3},{3,4},{4,5},{5,6},{6,7},{7,8},{8,9},{9,10},{10,1... | collective-permute-start | bytes 32 | tf_op jit(solution)/shard_map/ppermute | solution.py:31
  57.3 2.2 %collective-permute-start.4 = (s32[2]{0:T(128)S(1)}, s32[2]{0:T(128)S(1)}, u32[]{:S(2)}, u32[]{:S(2)}) collective-permute-start(s32[2]{0:T(128)S(1)} %collective-permute-done.2), channel_id=1, source_target_pairs={{0,1},{1,2},{2,3},{3,4},{4,5},{5,6},{6,7},{7,8},{8,9},{9,10},{10,1... | collective-permute-start | bytes 32 | tf_op jit(solution)/shard_map/ppermute | solution.py:31
  60.9 2.5 %select_select_fusion = (s32[256]{0:T(256)S(1)}, s32[256]{0:T(256)S(1)}) fusion(s32[]{:T(128)} %bitcast.23, s32[]{:T(128)} %bitcast.22, s32[]{:T(128)} %bitcast.19, s32[]{:T(128)} %bitcast.18), kind=kLoop, calls=%fused_computation.162 | loop fusion | flops 3328 | bytes 2064 | tf_op jit(solution)/shard_map/jit(_take)/select_n | solution.py:65
  64.1 1.8 %fusion.105 = (f32[8,256]{1,0:T(8,128)S(1)}, f32[8,256,256]{1,2,0:T(8,128)}) fusion(bf16[256,8,128]{0,2,1:T(8,128)(2,1)S(1)} %bitcast.267, bf16[256,512]{1,0:T(8,128)(2,1)S(1)} %copy-done.16, pred[256,256]{0,1:T(8,128)(4,1)S(1)} %get-tuple-element.161), kind=kOutput, calls=%fused_computation.183 | convolution fusion | flops 135788544 | bytes 2760704 | tf_op jit(solution)/shard_map/sjd,td->jst/dot_general | solution.py:39
  69.1 3.7 %collective-permute-start.3 = (bf16[256,512]{1,0:T(8,128)(2,1)}, bf16[256,512]{1,0:T(8,128)(2,1)S(1)}, u32[]{:S(2)}, u32[]{:S(2)}) collective-permute-start(bf16[256,512]{1,0:T(8,128)(2,1)} %collective-permute-done.1), channel_id=1, source_target_pairs={{0,1},{1,2},{2,3},{3,4},{4,5},{5,6},{6,7},{7,8},{8,9},{9,10},{10,1... | collective-permute-start | bytes 786440 | tf_op jit(solution)/shard_map/ppermute | solution.py:31
  74.1 2.6 %fusion.106 = (f32[8,256]{1,0:T(8,128)S(1)}, f32[8,256,256]{1,2,0:T(8,128)}) fusion(bf16[256,8,128]{0,2,1:T(8,128)(2,1)S(1)} %bitcast.269, bf16[256,512]{1,0:T(8,128)(2,1)} %collective-permute-done.1, pred[256,256]{0,1:T(8,128)(4,1)S(1)} %get-tuple-element.158), kind=kOutput, calls=%fused_computation.184 | convolution fusion | flops 135788544 | bytes 2760704 | tf_op jit(solution)/shard_map/sjd,td->jst/dot_general | solution.py:39
  76.7 2.6 %fusion.102 = (f32[8,256]{1,0:T(8,128)S(1)}, f32[8,256,256]{1,2,0:T(8,128)}) fusion(bf16[256,8,128]{0,2,1:T(8,128)(2,1)S(1)} %bitcast.264, bf16[256,512]{1,0:T(8,128)(2,1)} %collective-permute-done.1, pred[256,256]{0,1:T(8,128)(4,1)S(1)} %get-tuple-element.158), kind=kOutput, calls=%fused_computation.180 | convolution fusion | flops 135788544 | bytes 2760704 | tf_op jit(solution)/shard_map/sjd,td->jst/dot_general | solution.py:39
  79.3 4.2 %collective-permute-start.7 = (bf16[256,512]{0,1:T(8,128)(2,1)}, bf16[256,512]{0,1:T(8,128)(2,1)S(1)}, u32[]{:S(2)}, u32[]{:S(2)}) collective-permute-start(bf16[256,512]{0,1:T(8,128)(2,1)} %collective-permute-done.6), channel_id=1, source_target_pairs={{0,1},{1,2},{2,3},{3,4},{4,5},{5,6},{6,7},{7,8},{8,9},{9,10},{10,1... | collective-permute-start | bytes 786440 | tf_op jit(solution)/shard_map/ppermute | solution.py:31
  83.5 2.6 %fusion.98 = (f32[8,256]{1,0:T(8,128)S(1)}, f32[8,256,256]{1,2,0:T(8,128)}) fusion(bf16[256,8,128]{0,2,1:T(8,128)(2,1)S(1)} %bitcast.260, bf16[256,512]{1,0:T(8,128)(2,1)} %collective-permute-done.1, pred[256,256]{0,1:T(8,128)(4,1)S(1)} %get-tuple-element.158), kind=kOutput, calls=%fused_computation.176 | convolution fusion | flops 135788544 | bytes 2760704 | tf_op jit(solution)/shard_map/sjd,td->jst/dot_general | solution.py:39
  86.1 1.9 %collective-permute-start.5 = (bf16[256,512]{1,0:T(8,128)(2,1)S(1)}, bf16[256,512]{1,0:T(8,128)(2,1)S(1)}, u32[]{:S(2)}, u32[]{:S(2)}) collective-permute-start(bf16[256,512]{1,0:T(8,128)(2,1)S(1)} %collective-permute-done.3), channel_id=1, source_target_pairs={{0,1},{1,2},{2,3},{3,4},{4,5},{5,6},{6,7},{7,8},{8,9},{9,10},{10,1... | collective-permute-start | bytes 786440 | tf_op jit(solution)/shard_map/ppermute | solution.py:31
  88.5 1.8 %fusion.104 = (f32[8,256]{1,0:T(8,128)S(1)}, f32[8,256,256]{1,2,0:T(8,128)}) fusion(bf16[256,8,128]{0,2,1:T(8,128)(2,1)S(1)} %bitcast.270, bf16[256,512]{1,0:T(8,128)(2,1)S(1)} %collective-permute-done.3, pred[256,256]{0,1:T(8,128)(4,1)S(1)} %get-tuple-element.159), kind=kOutput, calls=%fused_computation.182 | convolution fusion | flops 135788544 | bytes 2760704 | tf_op jit(solution)/shard_map/sjd,td->jst/dot_general | solution.py:39
  90.3 1.8 %fusion.100 = (f32[8,256]{1,0:T(8,128)S(1)}, f32[8,256,256]{1,2,0:T(8,128)}) fusion(bf16[256,8,128]{0,2,1:T(8,128)(2,1)S(1)} %bitcast.265, bf16[256,512]{1,0:T(8,128)(2,1)S(1)} %collective-permute-done.3, pred[256,256]{0,1:T(8,128)(4,1)S(1)} %get-tuple-element.159), kind=kOutput, calls=%fused_computation.178 | convolution fusion | flops 135788544 | bytes 2760704 | tf_op jit(solution)/shard_map/sjd,td->jst/dot_general | solution.py:39
  92.1 4.8 %collective-permute-start.8 = (bf16[256,512]{0,1:T(8,128)(2,1)S(1)}, bf16[256,512]{0,1:T(8,128)(2,1)S(1)}, u32[]{:S(2)}, u32[]{:S(2)}) collective-permute-start(bf16[256,512]{0,1:T(8,128)(2,1)S(1)} %collective-permute-done.7), channel_id=1, source_target_pairs={{0,1},{1,2},{2,3},{3,4},{4,5},{5,6},{6,7},{7,8},{8,9},{9,10},{10,1... | collective-permute-start | bytes 786440 | tf_op jit(solution)/shard_map/ppermute | solution.py:31
  104.7 2.1 %copy.71 = bf16[256,1024]{1,0:T(8,128)(2,1)} copy(bf16[256,1024]{0,1:T(8,128)(2,1)} %bitcast.276) | data formatting | bytes 1048576 | tf_op jit(solution)/shard_map/reshape | solution.py:88
  110.1 3.1 %fusion.10 = (f32[8,256]{1,0:T(8,128)S(1)}, f32[8,256]{1,0:T(8,128)S(1)}, f32[8,256]{1,0:T(8,128)S(1)}, f32[8,256]{1,0:T(8,128)S(1)}) fusion(f32[8,256,256]{1,2,0:T(8,128)S(1)} %copy-done.6, f32[8,256]{1,0:T(8,128)S(1)} %maximum_maximum_fusion.2, f32[8,256,256]{1,2,0:T(8,128)S(1)} %copy-done.4, f32[8,256,256]{1,2,0:T(8,128)} %get-tuple-element.189, ...), kind=kLoop, calls=%fused_computation.44 | loop fusion | flops 4186112 | bytes 8429568 | tf_op jit(solution)/shard_map/reduce_sum | solution.py:85
  116.1 2.3 %fusion.41 = bf16[256,8,128]{0,2,1:T(8,128)(2,1)} fusion(f32[8,256,128]{1,2,0:T(8,128)S(1)} %convolution_add_fusion.7, f32[8,256,256]{1,2,0:T(8,128)S(1)} %get-tuple-element.187, f32[8,256]{1,0:T(8,128)S(1)} %maximum_maximum_fusion.2, f32[256,8]{0,1:T(8,128)S(1)} %add_bitcast_fusion.2, bf16[256,512]{0,1:T(8,128)(2,1)} %copy-done.18), kind=kOutput, calls=%fused_computation.87 | convolution fusion | flops 136052736 | bytes 3751936 | tf_op jit(solution)/shard_map/jst,td->sjd/dot_general | solution.py:46
  118.4 2.1 %copy.72 = bf16[256,1024]{1,0:T(8,128)(2,1)} copy(bf16[256,1024]{0,1:T(8,128)(2,1)} %bitcast.277) | data formatting | bytes 1048576 | tf_op jit(solution)/shard_map/reshape | solution.py:88
  123.6 3.1 %fusion.18 = (f32[8,256]{1,0:T(8,128)S(1)}, f32[8,256]{1,0:T(8,128)S(1)}, f32[8,256]{1,0:T(8,128)S(1)}, f32[8,256]{1,0:T(8,128)S(1)}) fusion(f32[8,256,256]{1,2,0:T(8,128)S(1)} %copy-done.3, f32[8,256]{1,0:T(8,128)S(1)} %maximum_maximum_fusion.1, f32[8,256,256]{1,2,0:T(8,128)S(1)} %copy-done.1, f32[8,256,256]{1,2,0:T(8,128)} %get-tuple-element.181, ...), kind=kLoop, calls=%fused_computation.52 | loop fusion | flops 4186112 | bytes 8429568 | tf_op jit(solution)/shard_map/reduce_sum | solution.py:85
  (117 shorter events, 59.8 us)
Async XLA Ops:
  39.2 11.9 %collective-permute-start = (s32[2]{0:T(128)S(1)}, s32[2]{0:T(128)S(1)}, u32[]{:S(2)}, u32[]{:S(2)}) collective-permute-start(s32[2]{0:T(128)S(1)} %add_bitcast_fusion.4), channel_id=1, source_target_pairs={{0,1},{1,2},{2,3},{3,4},{4,5},{5,6},{6,7},{7,8},{8,9},{9,10},{10,1... | collective-permute-start | bytes 32 | tf_op jit(solution)/shard_map/ppermute | solution.py:31
  40.5 28.6 %collective-permute-start.1 = (bf16[256,512]{1,0:T(8,128)(2,1)}, bf16[256,512]{1,0:T(8,128)(2,1)}, u32[]{:S(2)}, u32[]{:S(2)}) collective-permute-start(bf16[256,512]{1,0:T(8,128)(2,1)} %param.19), channel_id=1, source_target_pairs={{0,1},{1,2},{2,3},{3,4},{4,5},{5,6},{6,7},{7,8},{8,9},{9,10},{10,1... | collective-permute-start | bytes 786440 | tf_op jit(solution)/shard_map/ppermute | solution.py:31
  45.8 33.5 %collective-permute-start.6 = (bf16[256,512]{0,1:T(8,128)(2,1)S(1)}, bf16[256,512]{0,1:T(8,128)(2,1)}, u32[]{:S(2)}, u32[]{:S(2)}) collective-permute-start(bf16[256,512]{0,1:T(8,128)(2,1)S(1)} %copy.35), channel_id=1, source_target_pairs={{0,1},{1,2},{2,3},{3,4},{4,5},{5,6},{6,7},{7,8},{8,9},{9,10},{10,1... | collective-permute-start | bytes 786440 | tf_op jit(solution)/shard_map/ppermute | solution.py:31
  50.2 13.4 %copy-start.16 = (bf16[256,512]{1,0:T(8,128)(2,1)S(1)}, bf16[256,512]{1,0:T(8,128)(2,1)}, u32[]{:S(2)}) copy-start(bf16[256,512]{1,0:T(8,128)(2,1)} %param.19) | copy-start | bytes 786436
  50.4 13.7 %copy-start.10 = (bf16[256,1024]{0,1:T(8,128)(2,1)}, bf16[256,1024]{0,1:T(8,128)(2,1)S(1)}, u32[]{:S(2)}) copy-start(bf16[256,1024]{0,1:T(8,128)(2,1)S(1)} %copy.107) | copy-start | bytes 1572868
  50.6 13.5 %copy-start.8 = (bf16[256,1024]{0,1:T(8,128)(2,1)}, bf16[256,1024]{0,1:T(8,128)(2,1)S(1)}, u32[]{:S(2)}) copy-start(bf16[256,1024]{0,1:T(8,128)(2,1)S(1)} %copy.108) | copy-start | bytes 1572868
  54.2 3.1 %collective-permute-start.2 = (s32[2]{0:T(128)S(1)}, s32[2]{0:T(128)S(1)}, u32[]{:S(2)}, u32[]{:S(2)}) collective-permute-start(s32[2]{0:T(128)S(1)} %collective-permute-done), channel_id=1, source_target_pairs={{0,1},{1,2},{2,3},{3,4},{4,5},{5,6},{6,7},{7,8},{8,9},{9,10},{10,1... | collective-permute-start | bytes 32 | tf_op jit(solution)/shard_map/ppermute | solution.py:31
  57.3 3.0 %collective-permute-start.4 = (s32[2]{0:T(128)S(1)}, s32[2]{0:T(128)S(1)}, u32[]{:S(2)}, u32[]{:S(2)}) collective-permute-start(s32[2]{0:T(128)S(1)} %collective-permute-done.2), channel_id=1, source_target_pairs={{0,1},{1,2},{2,3},{3,4},{4,5},{5,6},{6,7},{7,8},{8,9},{9,10},{10,1... | collective-permute-start | bytes 32 | tf_op jit(solution)/shard_map/ppermute | solution.py:31
  66.0 6.8 %copy-start.11 = (bf16[256,1024]{0,1:T(8,128)(2,1)S(1)}, bf16[256,1024]{0,1:T(8,128)(2,1)}, u32[]{:S(2)}) copy-start(bf16[256,1024]{0,1:T(8,128)(2,1)} %copy-done.10) | copy-start | bytes 1572868
  67.7 6.4 %copy-start.9 = (bf16[256,1024]{0,1:T(8,128)(2,1)S(1)}, bf16[256,1024]{0,1:T(8,128)(2,1)}, u32[]{:S(2)}) copy-start(bf16[256,1024]{0,1:T(8,128)(2,1)} %copy-done.8) | copy-start | bytes 1572868
  69.1 17.1 %collective-permute-start.3 = (bf16[256,512]{1,0:T(8,128)(2,1)}, bf16[256,512]{1,0:T(8,128)(2,1)S(1)}, u32[]{:S(2)}, u32[]{:S(2)}) collective-permute-start(bf16[256,512]{1,0:T(8,128)(2,1)} %collective-permute-done.1), channel_id=1, source_target_pairs={{0,1},{1,2},{2,3},{3,4},{4,5},{5,6},{6,7},{7,8},{8,9},{9,10},{10,1... | collective-permute-start | bytes 786440 | tf_op jit(solution)/shard_map/ppermute | solution.py:31
  79.3 12.8 %collective-permute-start.7 = (bf16[256,512]{0,1:T(8,128)(2,1)}, bf16[256,512]{0,1:T(8,128)(2,1)S(1)}, u32[]{:S(2)}, u32[]{:S(2)}) collective-permute-start(bf16[256,512]{0,1:T(8,128)(2,1)} %collective-permute-done.6), channel_id=1, source_target_pairs={{0,1},{1,2},{2,3},{3,4},{4,5},{5,6},{6,7},{7,8},{8,9},{9,10},{10,1... | collective-permute-start | bytes 786440 | tf_op jit(solution)/shard_map/ppermute | solution.py:31
  86.1 12.6 %collective-permute-start.5 = (bf16[256,512]{1,0:T(8,128)(2,1)S(1)}, bf16[256,512]{1,0:T(8,128)(2,1)S(1)}, u32[]{:S(2)}, u32[]{:S(2)}) collective-permute-start(bf16[256,512]{1,0:T(8,128)(2,1)S(1)} %collective-permute-done.3), channel_id=1, source_target_pairs={{0,1},{1,2},{2,3},{3,4},{4,5},{5,6},{6,7},{7,8},{8,9},{9,10},{10,1... | collective-permute-start | bytes 786440 | tf_op jit(solution)/shard_map/ppermute | solution.py:31
  92.1 10.7 %copy-start.15 = (bf16[256,512]{0,1:T(8,128)(2,1)}, bf16[256,512]{0,1:T(8,128)(2,1)S(1)}, u32[]{:S(2)}) copy-start(bf16[256,512]{0,1:T(8,128)(2,1)S(1)} %collective-permute-done.7) | copy-start | bytes 786436
  92.1 11.2 %collective-permute-start.8 = (bf16[256,512]{0,1:T(8,128)(2,1)S(1)}, bf16[256,512]{0,1:T(8,128)(2,1)S(1)}, u32[]{:S(2)}, u32[]{:S(2)}) collective-permute-start(bf16[256,512]{0,1:T(8,128)(2,1)S(1)} %collective-permute-done.7), channel_id=1, source_target_pairs={{0,1},{1,2},{2,3},{3,4},{4,5},{5,6},{6,7},{7,8},{8,9},{9,10},{10,1... | collective-permute-start | bytes 786440 | tf_op jit(solution)/shard_map/ppermute | solution.py:31
  106.8 1.8 %copy-start.4 = (f32[8,256,256]{1,2,0:T(8,128)S(1)}, f32[8,256,256]{1,2,0:T(8,128)}, u32[]{:S(2)}) copy-start(f32[8,256,256]{1,2,0:T(8,128)} %get-tuple-element.191) | copy-start | bytes 6291460
  113.2 1.6 %copy-start.7 = (f32[8,256,256]{1,2,0:T(8,128)S(1)}, f32[8,256,256]{1,2,0:T(8,128)}, u32[]{:S(2)}) copy-start(f32[8,256,256]{1,2,0:T(8,128)} %get-tuple-element.189) | copy-start | bytes 6291460
  120.5 1.6 %copy-start.1 = (f32[8,256,256]{1,2,0:T(8,128)S(1)}, f32[8,256,256]{1,2,0:T(8,128)}, u32[]{:S(2)}) copy-start(f32[8,256,256]{1,2,0:T(8,128)} %get-tuple-element.183) | copy-start | bytes 6291460
  121.9 1.6 %copy-start.3 = (f32[8,256,256]{1,2,0:T(8,128)S(1)}, f32[8,256,256]{1,2,0:T(8,128)}, u32[]{:S(2)}) copy-start(f32[8,256,256]{1,2,0:T(8,128)} %get-tuple-element.185) | copy-start | bytes 6291460
  126.6 1.6 %copy-start.5 = (f32[8,256,256]{1,2,0:T(8,128)S(1)}, f32[8,256,256]{1,2,0:T(8,128)}, u32[]{:S(2)}) copy-start(f32[8,256,256]{1,2,0:T(8,128)} %get-tuple-element.181) | copy-start | bytes 6291460
  132.0 2.2 %copy-start.2 = (f32[8,256,256]{1,2,0:T(8,128)S(1)}, f32[8,256,256]{1,2,0:T(8,128)}, u32[]{:S(2)}) copy-start(f32[8,256,256]{1,2,0:T(8,128)} %get-tuple-element.173) | copy-start | bytes 6291460
  139.5 1.7 %copy-start.12 = (bf16[256,1024]{1,0:T(8,128)(2,1)S(1)}, bf16[256,1024]{1,0:T(8,128)(2,1)}, u32[]{:S(2)}) copy-start(bf16[256,1024]{1,0:T(8,128)(2,1)} %copy.71) | copy-start | bytes 1572868
  139.5 1.7 %copy-start.13 = (bf16[256,1024]{1,0:T(8,128)(2,1)S(1)}, bf16[256,1024]{1,0:T(8,128)(2,1)}, u32[]{:S(2)}) copy-start(bf16[256,1024]{1,0:T(8,128)(2,1)} %copy.72) | copy-start | bytes 1572868
  139.5 1.7 %copy-start.14 = (bf16[256,1024]{1,0:T(8,128)(2,1)S(1)}, bf16[256,1024]{1,0:T(8,128)(2,1)}, u32[]{:S(2)}) copy-start(bf16[256,1024]{1,0:T(8,128)(2,1)} %copy.73) | copy-start | bytes 1572868
  (4 other events, 5.2 us)
where the time goes:
time: 144 us; the launch traced here: 143 us
  matrix products  44.3 us (31%)
  local copies, waits for them, and re-layouts  27.8 us (19%)
  starting transfers between devices  26.6 us (18%)
  other arithmetic  18.1 us (13%)
  blocking collectives  13.7 us (10%)
  loops' own time  10.7 us (7%)
    ppermute x9, starting transfers between devices, passed_along(): lax.ppermute(value, axis, [(source, source + steps) for source in range(l...  26.6 us
    dot_general x16, matrix products, score_round(): jnp.einsum('sjd,td->jst', q_group, k_round, preferred_element_type=jnp.fl...  25.7 us
    dot_general x16, matrix products, mix_round(): jnp.einsum('jst,td->sjd', rounded, v_round, preferred_element_type=jnp.fl...  18.6 us
    unnamed x1, blocking collectives  13.7 us
    another operation x1, loops' own time, carried_in(): return lax.fori_loop(0, count - 1, lap, running)  10.7 us
    dynamic_slice x15, local copies, waits for them, and re-layouts, lap(): longer = join(running, pieces[position])  9.97 us
    reduce_sum x4, other arithmetic, per_device(): total = total + jnp.sum(weights, axis=2)  9.11 us
    unnamed x46, local copies, waits for them, and re-layouts  8.23 us
  transfers between devices with their start and end apart: 9, of which 2 were waited for; matrix products, arithmetic and copies ran while one was open for 25% of the time, Pallas kernels for 0%

commit v1 on v0

v1 whole, which is shorter than its diff:
```python
import functools
import math

import jax
import jax.numpy as jnp
from jax import lax
from jax.experimental import pallas as pl
from jax.experimental.pallas import tpu as pltpu
from jax.sharding import PartitionSpec as P

HD = 128
KVH = 4
GROUP = 8
BLK = 128
BACK = 5
NEG_FILL = -1e30
SCALE2 = math.log2(math.e) / math.sqrt(HD)
MESH = pl.DeviceIdType.MESH
HEADS_AT_ONCE = 2

ROWS = {3: (0, BLK), 2: (BLK, 2 * BLK), 1: (3 * BLK, 2 * BLK), 0: (5 * BLK, 2 * BLK)}
WINDOW = 7 * BLK
REACH = 6 * BLK


def kernel(
    n, q_hbm, k_hbm, v_hbm, flags_ref, o_hbm,
    q_buf, k_win, v_win, o_buf, bias, flags_out, flags_in,
    q_sem, own_sem, o_sem, send_sem, recv_sem, fwd_sem, fsend_sem, frecv_sem,
):
    me = lax.axis_index("ctx")
    core = lax.rem(me, 2)
    even, odd = core == 0, core == 1

    def window(win, g, back):
        start, size = ROWS[back]
        return win.at[g, pl.ds(start, size), :]

    def columns(g):
        return pl.ds(pl.multiple_of(g * HD, HD), HD)

    def q_copy(g):
        cols = pl.ds(pl.multiple_of(g * GROUP * HD, GROUP * HD), GROUP * HD)
        return pltpu.make_async_copy(q_hbm.at[:, cols], q_buf.at[g], q_sem.at[g])

    def o_copy(g):
        cols = pl.ds(pl.multiple_of(g * GROUP * HD, GROUP * HD), GROUP * HD)
        return pltpu.make_async_copy(o_buf.at[g], o_hbm.at[:, cols], o_sem.at[g])

    def own_copies(g):
        return [
            pltpu.make_async_copy(src.at[:, columns(g)], window(win, g, 0), own_sem.at[g, kv])
            for kv, (src, win) in enumerate(((k_hbm, k_win), (v_hbm, v_win)))
        ]

    def sends(g, back):
        size = ROWS[back][1]
        return [
            pltpu.make_async_remote_copy(
                src_ref=src.at[pl.ds(2 * BLK - size, size), columns(g)],
                dst_ref=window(win, g, back),
                send_sem=send_sem.at[g, back - 1, kv],
                recv_sem=recv_sem.at[g, back - 1, kv],
                device_id={"ctx": me + back},
                device_id_type=MESH,
            )
            for kv, (src, win) in enumerate(((k_hbm, k_win), (v_hbm, v_win)))
        ]

    def forwards(g, back):
        start, whole = ROWS[back]
        size = ROWS[back + 1][1]
        return [
            pltpu.make_async_remote_copy(
                src_ref=win.at[g, pl.ds(start + whole - size, size), :],
                dst_ref=window(win, g, back + 1),
                send_sem=fwd_sem.at[g, back - 1, kv],
                recv_sem=recv_sem.at[g, back, kv],
                device_id={"ctx": me + 1},
                device_id_type=MESH,
            )
            for kv, win in enumerate((k_win, v_win))
        ]

    def flag_send(back):
        return pltpu.make_async_remote_copy(
            src_ref=flags_out,
            dst_ref=flags_in.at[back - 1],
            send_sem=fsend_sem.at[back - 1],
            recv_sem=frecv_sem.at[back - 1],
            device_id={"ctx": me + back},
            device_id_type=MESH,
        )

    can_send = {
        1: me + 1 < n,
        2: even & (me + 2 < n),
        3: odd & (me + 3 < n),
    }
    direct = {1: me >= 1, 2: even & (me >= 2), 3: even & (me >= 3)}
    present = {back: me >= back for back in (1, 2, 3)}

    barrier = pltpu.get_barrier_semaphore()
    greet = [
        (1, me + 1 < n), (2, me + 2 < n), (3, can_send[3]),
        (-1, me >= 1), (-2, me >= 2), (-3, direct[3]),
    ]
    for step, there in greet:
        @pl.when(there)
        def _():
            pl.semaphore_signal(barrier, inc=1, device_id={"ctx": me + step}, device_id_type=MESH)

    for g in range(KVH):
        for copy in own_copies(g):
            copy.start()
        q_copy(g).start()
    flags_out[0:1, :] = jnp.full((1, BLK), flags_ref[0], jnp.int32)
    flags_out[1:2, :] = jnp.full((1, BLK), flags_ref[1], jnp.int32)
    flags_out[2:8, :] = jnp.zeros((6, BLK), jnp.int32)

    for back in (1, 2, 3):
        @pl.when(jnp.logical_not(present[back]))
        def _():
            start, size = ROWS[back]
            for win in (k_win, v_win):
                win[:, start:start + size, :] = jnp.zeros((KVH, size, HD), jnp.bfloat16)
            if back < 3:
                flags_in[back - 1] = jnp.zeros((8, BLK), jnp.int32)

    peers = jnp.int32(0)
    for _, there in greet:
        peers = peers + jnp.where(there, 1, 0)
    pl.semaphore_wait(barrier, peers)

    for back in (1, 2):
        @pl.when(me + back < n)
        def _():
            flag_send(back).start()
    for g in range(KVH):
        for back in (1, 2, 3):
            @pl.when(can_send[back])
            def _():
                for copy in sends(g, back):
                    copy.start()

    for back in (1, 2):
        @pl.when(present[back])
        def _():
            flag_send(back).wait_recv()

    mine = flags_out[...]
    begins = {0: mine[0:1], 1: mine[1:2]}
    for back in (1, 2):
        got = flags_in[back - 1]
        begins[-2 * back], begins[1 - 2 * back] = got[0:1], got[1:2]
    key_at = lax.broadcasted_iota(jnp.int32, (BLK, BLK), 0)
    row_at = lax.broadcasted_iota(jnp.int32, (BLK, BLK), 1)
    causal = jnp.where(key_at <= row_at, 0.0, NEG_FILL).astype(jnp.bfloat16)
    eye = (key_at == row_at).astype(jnp.bfloat16)
    for i in range(2):
        bias[i, BACK * BLK:(BACK + 1) * BLK, :] = causal
        hidden = jnp.zeros((1, BLK), jnp.float32)
        for b in range(i - 1, i - BACK - 1, -1):
            hidden = jnp.where(begins[b + 1] != 0, NEG_FILL, hidden)
            at = (b - i + BACK) * BLK
            bias[i, at:at + BLK, :] = jnp.broadcast_to(hidden, (BLK, BLK)).astype(jnp.bfloat16)
    ones = jnp.ones((REACH, HD), jnp.bfloat16)

    def one_group(g, carry):
        for back in (1, 2, 3):
            @pl.when(direct[back])
            def _():
                for copy in sends(g, back):
                    copy.wait_recv()
            if back < 3:
                @pl.when(even & present[back])
                def _():
                    for copy in forwards(g, back):
                        copy.start()
        for back in (2, 3):
            @pl.when(odd & present[back])
            def _():
                for copy in forwards(g, back - 1):
                    copy.wait_recv()
        for copy in own_copies(g):
            copy.wait()
        q_copy(g).wait()

        def some_heads(step, carry):
            for j in range(HEADS_AT_ONCE):
                cols = pl.ds(pl.multiple_of((step * HEADS_AT_ONCE + j) * HD, HD), HD)
                for i in range(2):
                    rows = pl.ds(i * BLK, BLK)
                    keys = pl.ds(i * BLK, REACH)
                    q = jnp.concatenate([q_buf[g, rows, cols], eye], axis=1)
                    k = jnp.concatenate([k_win[g, keys, :], bias[i]], axis=1)
                    s = lax.dot_general(
                        q, k, (((1,), (1,)), ((), ())), preferred_element_type=jnp.float32
                    )
                    top = jnp.max(s, axis=1, keepdims=True) * SCALE2
                    w = jnp.exp2(s * SCALE2 - top).astype(jnp.bfloat16)
                    v = jnp.concatenate([v_win[g, keys, :], ones], axis=1)
                    mixed = jnp.dot(w, v, preferred_element_type=jnp.float32)
                    o_buf[g, rows, cols] = (mixed[:, :HD] / mixed[:, HD:]).astype(jnp.bfloat16)
            return carry

        lax.fori_loop(0, GROUP // HEADS_AT_ONCE, some_heads, 0)
        o_copy(g).start()
        return carry

    lax.fori_loop(0, KVH, one_group, 0)

    for back in (1, 2):
        @pl.when(me + back < n)
        def _():
            flag_send(back).wait_send()
    for g in range(KVH):
        for back in (1, 2, 3):
            @pl.when(can_send[back])
            def _():
                for copy in sends(g, back):
                    copy.wait_send()
            if back < 3:
                @pl.when(even & present[back])
                def _():
                    for copy in forwards(g, back):
                        copy.wait_send()
        o_copy(g).wait()


def per_device(n, queries, keys, values, doc_flags):
    rows = queries.shape[0]
    dma = pltpu.SemaphoreType.DMA
    return pl.pallas_call(
        functools.partial(kernel, n),
        out_shape=jax.ShapeDtypeStruct(queries.shape, jnp.bfloat16),
        in_specs=[pl.BlockSpec(memory_space=pl.ANY)] * 3 + [pl.BlockSpec(memory_space=pltpu.SMEM)],
        out_specs=pl.BlockSpec(memory_space=pl.ANY),
        scratch_shapes=[
            pltpu.VMEM((KVH, rows, GROUP * HD), jnp.bfloat16),
            pltpu.VMEM((KVH, WINDOW, HD), jnp.bfloat16),
            pltpu.VMEM((KVH, WINDOW, HD), jnp.bfloat16),
            pltpu.VMEM((KVH, rows, GROUP * HD), jnp.bfloat16),
            pltpu.VMEM((2, REACH, BLK), jnp.bfloat16),
            pltpu.VMEM((8, BLK), jnp.int32),
            pltpu.VMEM((2, 8, BLK), jnp.int32),
            dma((KVH,)),
            dma((KVH, 2)),
            dma((KVH,)),
            dma((KVH, 3, 2)),
            dma((KVH, 3, 2)),
            dma((KVH, 2, 2)),
            dma((2,)),
            dma((2,)),
        ],
        compiler_params=pltpu.CompilerParams(
            collective_id=0, has_side_effects=True, vmem_limit_bytes=40 * 1024 * 1024
        ),
        name="window_attention",
    )(queries, keys, values, doc_flags)


def solution(mesh):
    spread = P(("groups", "ctx"), None)
    return jax.shard_map(
        functools.partial(per_device, mesh.shape["ctx"]),
        mesh=mesh,
        in_specs=(spread, spread, spread, P(("groups", "ctx"))),
        out_specs=spread,
        check_vma=False,
    )
```

time: 144 us -> 43.1 us (0.30)
  the two profiles are of different devices: /device:TPU:0 before, /device:TPU:21 now
where the time goes in v1:
time: 43.1 us; the launch traced here: 42.5 us
  Pallas kernels  37 us (86%)
  local copies, waits for them, and re-layouts  5.47 us (13%)
    pallas_call x1, Pallas kernels, per_device(): pl.pallas_call(functools.partial(kernel, n), out_shape=jax.ShapeDtypeStru...  37 us
    unnamed x9, local copies, waits for them, and re-layouts  5.47 us

profile of v1, /device:TPU:21, one launch (start us, length us, event | category | flops | bytes accessed | tf_op | source)
XLA Modules:
  0.0 42.5 jit_solution(10775912633511473527)
XLA Ops:
  0.0 0.0 copy-start
  0.0 1.6 %copy-done = bf16[256,4096]{1,0:T(8,128)(2,1)S(1)} copy-done((bf16[256,4096]{1,0:T(8,128)(2,1)S(1)}, bf16[256,4096]{1,0:T(8,128)(2,1)}, u32[]{:S(2)}) %copy-start) | copy-done | bytes 2097176
  1.6 0.0 copy-start.1
  1.6 0.9 %copy-done.1 = bf16[256,512]{1,0:T(8,128)(2,1)S(1)} copy-done((bf16[256,512]{1,0:T(8,128)(2,1)S(1)}, bf16[256,512]{1,0:T(8,128)(2,1)}, u32[]{:S(2)}) %copy-start.1) | copy-done | bytes 262168
  2.5 0.0 copy-start.2
  2.5 0.9 %copy-done.2 = bf16[256,512]{1,0:T(8,128)(2,1)S(1)} copy-done((bf16[256,512]{1,0:T(8,128)(2,1)S(1)}, bf16[256,512]{1,0:T(8,128)(2,1)}, u32[]{:S(2)}) %copy-start.2) | copy-done | bytes 262168
  3.5 0.0 copy-start.3
  3.5 0.7 %copy-done.3 = s32[2]{0:T(128)S(1)} copy-done((s32[2]{0:T(128)S(1)}, s32[2]{0:T(128)}, u32[]{:S(2)}) %copy-start.3) | copy-done | bytes 32
  4.1 37.0 %window_attention.1 = bf16[256,4096]{1,0:T(8,128)(2,1)S(1)} custom-call(bf16[256,4096]{1,0:T(8,128)(2,1)S(1)} %copy-done, bf16[256,512]{1,0:T(8,128)(2,1)S(1)} %copy-done.1, bf16[256,512]{1,0:T(8,128)(2,1)S(1)} %copy-done.2, s32[2]{0:T(128)S(1)} %copy-done.3), custom_call_target="tpu_custom_call" | custom-call | tf_op jit(solution)/shard_map/window_attention/pallas_call | solution.py:234
  41.2 1.3 %copy.6 = bf16[256,4096]{1,0:T(8,128)(2,1)} copy(bf16[256,4096]{1,0:T(8,128)(2,1)S(1)} %window_attention.1) | data formatting | bytes 4194304
Async XLA Ops:
  0.0 1.6 %copy-start = (bf16[256,4096]{1,0:T(8,128)(2,1)S(1)}, bf16[256,4096]{1,0:T(8,128)(2,1)}, u32[]{:S(2)}) copy-start(bf16[256,4096]{1,0:T(8,128)(2,1)} %q_hbm.1) | copy-start | bytes 6291460
  1.6 0.9 %copy-start.1 = (bf16[256,512]{1,0:T(8,128)(2,1)S(1)}, bf16[256,512]{1,0:T(8,128)(2,1)}, u32[]{:S(2)}) copy-start(bf16[256,512]{1,0:T(8,128)(2,1)} %k_hbm.1) | copy-start | bytes 786436
  2.5 0.9 %copy-start.2 = (bf16[256,512]{1,0:T(8,128)(2,1)S(1)}, bf16[256,512]{1,0:T(8,128)(2,1)}, u32[]{:S(2)}) copy-start(bf16[256,512]{1,0:T(8,128)(2,1)} %v_hbm.1) | copy-start | bytes 786436
  3.5 0.7 %copy-start.3 = (s32[2]{0:T(128)S(1)}, s32[2]{0:T(128)}, u32[]{:S(2)}) copy-start(s32[2]{0:T(128)} %flags_ref.1) | copy-start | bytes 28

commit v2 on v1

--- a/solution.py
+++ b/solution.py
@@ -16,7 +16,6 @@
 NEG_FILL = -1e30
 SCALE2 = math.log2(math.e) / math.sqrt(HD)
 MESH = pl.DeviceIdType.MESH
-HEADS_AT_ONCE = 2
 
 ROWS = {3: (0, BLK), 2: (BLK, 2 * BLK), 1: (3 * BLK, 2 * BLK), 0: (5 * BLK, 2 * BLK)}
 WINDOW = 7 * BLK
@@ -186,25 +185,25 @@
             copy.wait()
         q_copy(g).wait()
 
-        def some_heads(step, carry):
-            for j in range(HEADS_AT_ONCE):
-                cols = pl.ds(pl.multiple_of((step * HEADS_AT_ONCE + j) * HD, HD), HD)
-                for i in range(2):
-                    rows = pl.ds(i * BLK, BLK)
-                    keys = pl.ds(i * BLK, REACH)
-                    q = jnp.concatenate([q_buf[g, rows, cols], eye], axis=1)
-                    k = jnp.concatenate([k_win[g, keys, :], bias[i]], axis=1)
-                    s = lax.dot_general(
-                        q, k, (((1,), (1,)), ((), ())), preferred_element_type=jnp.float32
-                    )
-                    top = jnp.max(s, axis=1, keepdims=True) * SCALE2
-                    w = jnp.exp2(s * SCALE2 - top).astype(jnp.bfloat16)
-                    v = jnp.concatenate([v_win[g, keys, :], ones], axis=1)
-                    mixed = jnp.dot(w, v, preferred_element_type=jnp.float32)
-                    o_buf[g, rows, cols] = (mixed[:, :HD] / mixed[:, HD:]).astype(jnp.bfloat16)
-            return carry
-
-        lax.fori_loop(0, GROUP // HEADS_AT_ONCE, some_heads, 0)
+        for i in range(2):
+            rows = pl.ds(i * BLK, BLK)
+            keys = pl.ds(i * BLK, REACH)
+            heads = [pl.ds(j * HD, HD) for j in range(GROUP)]
+            q = jnp.concatenate(
+                [jnp.concatenate([q_buf[g, rows, head], eye], axis=1) for head in heads], axis=0
+            )
+            k = jnp.concatenate([k_win[g, keys, :], bias[i]], axis=1)
+            s = lax.dot_general(
+                q, k, (((1,), (1,)), ((), ())), preferred_element_type=jnp.float32
+            )
+            top = jnp.max(s, axis=1, keepdims=True) * SCALE2
+            w = jnp.exp2(s * SCALE2 - top).astype(jnp.bfloat16)
+            v = jnp.concatenate([v_win[g, keys, :], ones], axis=1)
+            mixed = jnp.dot(w, v, preferred_element_type=jnp.float32)
+            out = (mixed[:, :HD] / mixed[:, HD:]).astype(jnp.bfloat16)
+            for j, head in enumerate(heads):
+                o_buf[g, rows, head] = out[j * BLK:(j + 1) * BLK]
+
         o_copy(g).start()
         return carry
 
@@ -254,7 +253,7 @@
             dma((2,)),
         ],
         compiler_params=pltpu.CompilerParams(
-            collective_id=0, has_side_effects=True, vmem_limit_bytes=40 * 1024 * 1024
+            collective_id=0, has_side_effects=True, vmem_limit_bytes=62 * 1024 * 1024
         ),
         name="window_attention",
     )(queries, keys, values, doc_flags)

time: 43.1 us -> 27.9 us (0.65); the launches traced: 42.5 us -> 27.8 us
  Pallas kernels: 37 us -> 24.7 us
  local copies, waits for them, and re-layouts: 5.47 us -> 3.13 us
    pallas_call x1, Pallas kernels: 37 us -> 24.7 us  [per_device(): pl.pallas_call(functools.partial(kernel, n), out_shape=jax.ShapeDtypeStru...]
    unnamed x9 -> x1, local copies, waits for them, and re-layouts: 5.47 us -> 3.13 us
where the time goes in v2:
time: 27.9 us; the launch traced here: 27.8 us
  Pallas kernels  24.7 us (89%)
  local copies, waits for them, and re-layouts  3.13 us (11%)
    pallas_call x1, Pallas kernels, per_device(): pl.pallas_call(functools.partial(kernel, n), out_shape=jax.ShapeDtypeStru...  24.7 us
    unnamed x1, local copies, waits for them, and re-layouts  3.13 us

profile of v2, /device:TPU:21, one launch (start us, length us, event | category | flops | bytes accessed | tf_op | source)
XLA Modules:
  0.0 27.8 jit_solution(10332167604894446252)
XLA Ops:
  0.0 24.7 %window_attention.1 = bf16[256,4096]{1,0:T(8,128)(2,1)} custom-call(bf16[256,4096]{1,0:T(8,128)(2,1)} %q_hbm.1, bf16[256,512]{1,0:T(8,128)(2,1)} %k_hbm.1, bf16[256,512]{1,0:T(8,128)(2,1)} %v_hbm.1, s32[2]{0:T(128)} %flags_ref.1), custom_call_target="tpu_custom_call" | custom-call | tf_op jit(solution)/shard_map/window_attention/pallas_call | solution.py:233
  24.7 3.1 %copy.6 = bf16[256,4096]{1,0:T(8,128)(2,1)} copy(bf16[256,4096]{1,0:T(8,128)(2,1)} %window_attention.1) | data formatting | bytes 4194304

commit v3 on v2

--- a/solution.py
+++ b/solution.py
@@ -22,10 +22,52 @@
 REACH = 6 * BLK
 
 
+def attend(i, q_ref, k_ref, v_ref, bias, o_ref):
+    rows, keys = pl.ds(i * BLK, BLK), pl.ds(i * BLK, REACH)
+    heads = [pl.ds(j * HD, HD) for j in range(GROUP)]
+    key_at = lax.broadcasted_iota(jnp.int32, (BLK, BLK), 0)
+    row_at = lax.broadcasted_iota(jnp.int32, (BLK, BLK), 1)
+    eye = (key_at == row_at).astype(jnp.bfloat16)
+    q = jnp.concatenate(
+        [jnp.concatenate([q_ref[rows, head], eye], axis=1) for head in heads], axis=0
+    )
+    k = jnp.concatenate([k_ref[keys, :], bias[i]], axis=1)
+    s = lax.dot_general(q, k, (((1,), (1,)), ((), ())), preferred_element_type=jnp.float32)
+    top = jnp.max(s, axis=1, keepdims=True) * SCALE2
+    w = jnp.exp2(s * SCALE2 - top).astype(jnp.bfloat16)
+    v = jnp.concatenate([v_ref[keys, :], jnp.ones((REACH, HD), jnp.bfloat16)], axis=1)
+    mixed = jnp.dot(w, v, preferred_element_type=jnp.float32)
+    out = (mixed[:, :HD] / mixed[:, HD:]).astype(jnp.bfloat16)
+    for j, head in enumerate(heads):
+        o_ref[rows, head] = out[j * BLK:(j + 1) * BLK]
+
+
+def last_kernel(o_first, q_buf, k_win, v_win, bias, o_hbm, o_buf, sem):
+    width, last = GROUP * HD, KVH - 1
+    moves = []
+    for g in range(last):
+        move = pltpu.make_async_copy(
+            o_first.at[g], o_hbm.at[:, pl.ds(g * width, width)], sem.at[g]
+        )
+        move.start()
+        moves.append(move)
+    for i in range(2):
+        attend(i, q_buf.at[last], k_win.at[last], v_win.at[last], bias, o_buf)
+        rows = pl.ds(i * BLK, BLK)
+        move = pltpu.make_async_copy(
+            o_buf.at[rows, :], o_hbm.at[rows, pl.ds(last * width, width)], sem.at[last + i]
+        )
+        move.start()
+        moves.append(move)
+    for move in moves:
+        move.wait()
+
+
 def kernel(
-    n, q_hbm, k_hbm, v_hbm, flags_ref, o_hbm,
-    q_buf, k_win, v_win, o_buf, bias, flags_out, flags_in,
-    q_sem, own_sem, o_sem, send_sem, recv_sem, fwd_sem, fsend_sem, frecv_sem,
+    n, q_hbm, k_hbm, v_hbm, flags_hbm,
+    o_buf, q_buf, k_win, v_win, bias,
+    flags_ref, flags_out, flags_in,
+    q_sem, own_sem, flag_sem, send_sem, recv_sem, fwd_sem, fsend_sem, frecv_sem,
 ):
     me = lax.axis_index("ctx")
     core = lax.rem(me, 2)
@@ -41,10 +83,6 @@
     def q_copy(g):
         cols = pl.ds(pl.multiple_of(g * GROUP * HD, GROUP * HD), GROUP * HD)
         return pltpu.make_async_copy(q_hbm.at[:, cols], q_buf.at[g], q_sem.at[g])
-
-    def o_copy(g):
-        cols = pl.ds(pl.multiple_of(g * GROUP * HD, GROUP * HD), GROUP * HD)
-        return pltpu.make_async_copy(o_buf.at[g], o_hbm.at[:, cols], o_sem.at[g])
 
     def own_copies(g):
         return [
@@ -99,6 +137,8 @@
     direct = {1: me >= 1, 2: even & (me >= 2), 3: even & (me >= 3)}
     present = {back: me >= back for back in (1, 2, 3)}
 
+    flag_copy = pltpu.make_async_copy(flags_hbm, flags_ref, flag_sem)
+    flag_copy.start()
     barrier = pltpu.get_barrier_semaphore()
     greet = [
         (1, me + 1 < n), (2, me + 2 < n), (3, can_send[3]),
@@ -113,6 +153,7 @@
         for copy in own_copies(g):
             copy.start()
         q_copy(g).start()
+    flag_copy.wait()
     flags_out[0:1, :] = jnp.full((1, BLK), flags_ref[0], jnp.int32)
     flags_out[1:2, :] = jnp.full((1, BLK), flags_ref[1], jnp.int32)
     flags_out[2:8, :] = jnp.zeros((6, BLK), jnp.int32)
@@ -155,7 +196,6 @@
     key_at = lax.broadcasted_iota(jnp.int32, (BLK, BLK), 0)
     row_at = lax.broadcasted_iota(jnp.int32, (BLK, BLK), 1)
     causal = jnp.where(key_at <= row_at, 0.0, NEG_FILL).astype(jnp.bfloat16)
-    eye = (key_at == row_at).astype(jnp.bfloat16)
     for i in range(2):
         bias[i, BACK * BLK:(BACK + 1) * BLK, :] = causal
         hidden = jnp.zeros((1, BLK), jnp.float32)
@@ -163,9 +203,7 @@
             hidden = jnp.where(begins[b + 1] != 0, NEG_FILL, hidden)
             at = (b - i + BACK) * BLK
             bias[i, at:at + BLK, :] = jnp.broadcast_to(hidden, (BLK, BLK)).astype(jnp.bfloat16)
-    ones = jnp.ones((REACH, HD), jnp.bfloat16)
-
-    def one_group(g, carry):
+    def arrive(g):
         for back in (1, 2, 3):
             @pl.when(direct[back])
             def _():
@@ -185,29 +223,14 @@
             copy.wait()
         q_copy(g).wait()
 
+    def one_group(g, carry):
+        arrive(g)
         for i in range(2):
-            rows = pl.ds(i * BLK, BLK)
-            keys = pl.ds(i * BLK, REACH)
-            heads = [pl.ds(j * HD, HD) for j in range(GROUP)]
-            q = jnp.concatenate(
-                [jnp.concatenate([q_buf[g, rows, head], eye], axis=1) for head in heads], axis=0
-            )
-            k = jnp.concatenate([k_win[g, keys, :], bias[i]], axis=1)
-            s = lax.dot_general(
-                q, k, (((1,), (1,)), ((), ())), preferred_element_type=jnp.float32
-            )
-            top = jnp.max(s, axis=1, keepdims=True) * SCALE2
-            w = jnp.exp2(s * SCALE2 - top).astype(jnp.bfloat16)
-            v = jnp.concatenate([v_win[g, keys, :], ones], axis=1)
-            mixed = jnp.dot(w, v, preferred_element_type=jnp.float32)
-            out = (mixed[:, :HD] / mixed[:, HD:]).astype(jnp.bfloat16)
-            for j, head in enumerate(heads):
-                o_buf[g, rows, head] = out[j * BLK:(j + 1) * BLK]
-
-        o_copy(g).start()
+            attend(i, q_buf.at[g], k_win.at[g], v_win.at[g], bias, o_buf.at[g])
         return carry
 
-    lax.fori_loop(0, KVH, one_group, 0)
+    lax.fori_loop(0, KVH - 1, one_group, 0)
+    arrive(KVH - 1)
 
     for back in (1, 2):
         @pl.when(me + back < n)
@@ -224,28 +247,33 @@
                 def _():
                     for copy in forwards(g, back):
                         copy.wait_send()
-        o_copy(g).wait()
 
 
 def per_device(n, queries, keys, values, doc_flags):
     rows = queries.shape[0]
     dma = pltpu.SemaphoreType.DMA
-    return pl.pallas_call(
+    inputs = [
+        pltpu.with_memory_space_constraint(x, pltpu.HBM)
+        for x in (queries, keys, values, doc_flags)
+    ]
+    staged = pl.pallas_call(
         functools.partial(kernel, n),
-        out_shape=jax.ShapeDtypeStruct(queries.shape, jnp.bfloat16),
-        in_specs=[pl.BlockSpec(memory_space=pl.ANY)] * 3 + [pl.BlockSpec(memory_space=pltpu.SMEM)],
-        out_specs=pl.BlockSpec(memory_space=pl.ANY),
-        scratch_shapes=[
+        out_shape=[
+            pltpu.VMEM((KVH - 1, rows, GROUP * HD), jnp.bfloat16),
             pltpu.VMEM((KVH, rows, GROUP * HD), jnp.bfloat16),
             pltpu.VMEM((KVH, WINDOW, HD), jnp.bfloat16),
             pltpu.VMEM((KVH, WINDOW, HD), jnp.bfloat16),
-            pltpu.VMEM((KVH, rows, GROUP * HD), jnp.bfloat16),
             pltpu.VMEM((2, REACH, BLK), jnp.bfloat16),
+        ],
+        in_specs=[pl.BlockSpec(memory_space=pltpu.HBM)] * 4,
+        out_specs=[pl.BlockSpec(memory_space=pltpu.VMEM)] * 5,
+        scratch_shapes=[
+            pltpu.SMEM(doc_flags.shape, jnp.int32),
             pltpu.VMEM((8, BLK), jnp.int32),
             pltpu.VMEM((2, 8, BLK), jnp.int32),
             dma((KVH,)),
             dma((KVH, 2)),
-            dma((KVH,)),
+            dma,
             dma((KVH, 3, 2)),
             dma((KVH, 3, 2)),
             dma((KVH, 2, 2)),
@@ -253,10 +281,19 @@
             dma((2,)),
         ],
         compiler_params=pltpu.CompilerParams(
-            collective_id=0, has_side_effects=True, vmem_limit_bytes=62 * 1024 * 1024
+            collective_id=0, has_side_effects=True, vmem_limit_bytes=32 * 1024 * 1024
         ),
         name="window_attention",
-    )(queries, keys, values, doc_flags)
+    )(*inputs)
+    return pl.pallas_call(
+        last_kernel,
+        out_shape=jax.ShapeDtypeStruct(queries.shape, jnp.bfloat16),
+        in_specs=[pl.BlockSpec(memory_space=pltpu.VMEM)] * 5,
+        out_specs=pl.BlockSpec(memory_space=pltpu.HBM),
+        scratch_shapes=[pltpu.VMEM((rows, GROUP * HD), jnp.bfloat16), dma((KVH + 1,))],
+        compiler_params=pltpu.CompilerParams(vmem_limit_bytes=32 * 1024 * 1024),
+        name="last_group",
+    )(*staged)
 
 
 def solution(mesh):

time: 27.9 us -> 24 us (0.86)
  local copies, waits for them, and re-layouts: 3.13 us -> 0 us
  Pallas kernels: 24.7 us -> 23.8 us
    unnamed x1 -> x0, local copies, waits for them, and re-layouts: 3.13 us -> none
    pallas_call x1 -> x2, Pallas kernels: 24.7 us -> 23.8 us  [the longest x1 20.3 us: per_device(): pl.pallas_call(functools.partial(kernel, n), out_shape=[pltpu.VMEM((KVH -...]
where the time goes in v3:
time: 24 us; the launch traced here: 23.8 us
  Pallas kernels  23.8 us (99%)
    pallas_call x1, Pallas kernels, per_device(): pl.pallas_call(functools.partial(kernel, n), out_shape=[pltpu.VMEM((KVH -...  20.3 us
    pallas_call x1, Pallas kernels, per_device(): pl.pallas_call(last_kernel, out_shape=jax.ShapeDtypeStruct(queries.shape,...  3.51 us

profile of v3, /device:TPU:21, one launch (start us, length us, event | category | flops | bytes accessed | tf_op | source)
XLA Modules:
  0.0 23.8 jit_solution(18137111914475433939)
XLA Ops:
  0.0 20.3 %window_attention.1 = (bf16[3,256,1024]{2,1,0:T(8,128)(2,1)S(1)}, bf16[4,256,1024]{2,1,0:T(8,128)(2,1)S(1)}, bf16[4,896,128]{2,1,0:T(8,128)(2,1)S(1)}, bf16[4,89...) custom-call(bf16[256,4096]{1,0:T(8,128)(2,1)} %q_hbm.1, bf16[256,512]{1,0:T(8,128)(2,1)} %k_hbm.1, bf16[256,512]{1,0:T(8,128)(2,1)} %v_hbm.1, ...), custom_call_target="tpu_custom_call" | custom-call | tf_op jit(solution)/shard_map/window_attention/pallas_call | solution.py:259
  20.3 3.5 %last_group.1 = bf16[256,4096]{1,0:T(8,128)(2,1)} custom-call(bf16[3,256,1024]{2,1,0:T(8,128)(2,1)S(1)} %get-tuple-element.10.o_first, bf16[4,256,1024]{2,1,0:T(8,128)(2,1)S(1)} %get-tuple-element.11.q_buf, bf16[4,896,128]{2,1,0:T(8,128)(2,1)S(1)} %get-tuple-element.12.k_win, bf16[4,896,128]{2,1,0:T(8,128)(2,1)S(1)} %get-tuple-element.13.v_win, ...), custom_call_target="tpu_custom_call" | custom-call | tf_op jit(solution)/shard_map/last_group/pallas_call | solution.py:288

commit v4 on v3

--- a/solution.py
+++ b/solution.py
@@ -16,33 +16,40 @@
 NEG_FILL = -1e30
 SCALE2 = math.log2(math.e) / math.sqrt(HD)
 MESH = pl.DeviceIdType.MESH
+SEND_ORDER = (1, 2, 3)
 
 ROWS = {3: (0, BLK), 2: (BLK, 2 * BLK), 1: (3 * BLK, 2 * BLK), 0: (5 * BLK, 2 * BLK)}
 WINDOW = 7 * BLK
 REACH = 6 * BLK
 
 
-def attend(i, q_ref, k_ref, v_ref, bias, o_ref):
+HEADS = [pl.ds(j * HD, HD) for j in range(GROUP)]
+
+
+def weigh(i, q_ref, k_ref, bias):
     rows, keys = pl.ds(i * BLK, BLK), pl.ds(i * BLK, REACH)
-    heads = [pl.ds(j * HD, HD) for j in range(GROUP)]
     key_at = lax.broadcasted_iota(jnp.int32, (BLK, BLK), 0)
     row_at = lax.broadcasted_iota(jnp.int32, (BLK, BLK), 1)
     eye = (key_at == row_at).astype(jnp.bfloat16)
     q = jnp.concatenate(
-        [jnp.concatenate([q_ref[rows, head], eye], axis=1) for head in heads], axis=0
+        [jnp.concatenate([q_ref[rows, head], eye], axis=1) for head in HEADS], axis=0
     )
     k = jnp.concatenate([k_ref[keys, :], bias[i]], axis=1)
     s = lax.dot_general(q, k, (((1,), (1,)), ((), ())), preferred_element_type=jnp.float32)
     top = jnp.max(s, axis=1, keepdims=True) * SCALE2
-    w = jnp.exp2(s * SCALE2 - top).astype(jnp.bfloat16)
+    return jnp.exp2(s * SCALE2 - top).astype(jnp.bfloat16)
+
+
+def mix(i, w, v_ref, o_ref):
+    rows, keys = pl.ds(i * BLK, BLK), pl.ds(i * BLK, REACH)
     v = jnp.concatenate([v_ref[keys, :], jnp.ones((REACH, HD), jnp.bfloat16)], axis=1)
     mixed = jnp.dot(w, v, preferred_element_type=jnp.float32)
     out = (mixed[:, :HD] / mixed[:, HD:]).astype(jnp.bfloat16)
-    for j, head in enumerate(heads):
+    for j, head in enumerate(HEADS):
         o_ref[rows, head] = out[j * BLK:(j + 1) * BLK]
 
 
-def last_kernel(o_first, q_buf, k_win, v_win, bias, o_hbm, o_buf, sem):
+def last_kernel(o_first, v_win, w_last, o_hbm, o_buf, sem):
     width, last = GROUP * HD, KVH - 1
     moves = []
     for g in range(last):
@@ -52,7 +59,7 @@
         move.start()
         moves.append(move)
     for i in range(2):
-        attend(i, q_buf.at[last], k_win.at[last], v_win.at[last], bias, o_buf)
+        mix(i, w_last[i], v_win.at[last], o_buf)
         rows = pl.ds(i * BLK, BLK)
         move = pltpu.make_async_copy(
             o_buf.at[rows, :], o_hbm.at[rows, pl.ds(last * width, width)], sem.at[last + i]
@@ -65,8 +72,8 @@
 
 def kernel(
     n, q_hbm, k_hbm, v_hbm, flags_hbm,
-    o_buf, q_buf, k_win, v_win, bias,
-    flags_ref, flags_out, flags_in,
+    o_buf, v_win, w_last,
+    q_buf, k_win, bias, flags_ref, flags_out, flags_in,
     q_sem, own_sem, flag_sem, send_sem, recv_sem, fwd_sem, fsend_sem, frecv_sem,
 ):
     me = lax.axis_index("ctx")
@@ -94,14 +101,14 @@
         size = ROWS[back][1]
         return [
             pltpu.make_async_remote_copy(
-                src_ref=src.at[pl.ds(2 * BLK - size, size), columns(g)],
+                src_ref=win.at[g, pl.ds(WINDOW - size, size), :],
                 dst_ref=window(win, g, back),
                 send_sem=send_sem.at[g, back - 1, kv],
                 recv_sem=recv_sem.at[g, back - 1, kv],
                 device_id={"ctx": me + back},
                 device_id_type=MESH,
             )
-            for kv, (src, win) in enumerate(((k_hbm, k_win), (v_hbm, v_win)))
+            for kv, win in enumerate((k_win, v_win))
         ]
 
     def forwards(g, back):
@@ -152,6 +159,7 @@
     for g in range(KVH):
         for copy in own_copies(g):
             copy.start()
+    for g in range(KVH):
         q_copy(g).start()
     flag_copy.wait()
     flags_out[0:1, :] = jnp.full((1, BLK), flags_ref[0], jnp.int32)
@@ -176,12 +184,15 @@
         @pl.when(me + back < n)
         def _():
             flag_send(back).start()
-    for g in range(KVH):
-        for back in (1, 2, 3):
+    batches = [(g, (0, 1)) for g in range(KVH - 1)] + [(KVH - 1, (0,)), (KVH - 1, (1,))]
+    for g, kinds in batches:
+        for kv in kinds:
+            own_copies(g)[kv].wait()
+        for back in SEND_ORDER:
             @pl.when(can_send[back])
             def _():
-                for copy in sends(g, back):
-                    copy.start()
+                for kv in kinds:
+                    sends(g, back)[kv].start()
 
     for back in (1, 2):
         @pl.when(present[back])
@@ -203,34 +214,39 @@
             hidden = jnp.where(begins[b + 1] != 0, NEG_FILL, hidden)
             at = (b - i + BACK) * BLK
             bias[i, at:at + BLK, :] = jnp.broadcast_to(hidden, (BLK, BLK)).astype(jnp.bfloat16)
-    def arrive(g):
+    def arrive(g, kinds=(0, 1)):
+        def pick(copies):
+            return [copies[kv] for kv in kinds]
+
         for back in (1, 2, 3):
             @pl.when(direct[back])
             def _():
-                for copy in sends(g, back):
+                for copy in pick(sends(g, back)):
                     copy.wait_recv()
             if back < 3:
                 @pl.when(even & present[back])
                 def _():
-                    for copy in forwards(g, back):
+                    for copy in pick(forwards(g, back)):
                         copy.start()
         for back in (2, 3):
             @pl.when(odd & present[back])
             def _():
-                for copy in forwards(g, back - 1):
+                for copy in pick(forwards(g, back - 1)):
                     copy.wait_recv()
-        for copy in own_copies(g):
-            copy.wait()
-        q_copy(g).wait()
+        if 0 in kinds:
+            q_copy(g).wait()
 
     def one_group(g, carry):
         arrive(g)
         for i in range(2):
-            attend(i, q_buf.at[g], k_win.at[g], v_win.at[g], bias, o_buf.at[g])
+            mix(i, weigh(i, q_buf.at[g], k_win.at[g], bias), v_win.at[g], o_buf.at[g])
         return carry
 
     lax.fori_loop(0, KVH - 1, one_group, 0)
-    arrive(KVH - 1)
+    arrive(KVH - 1, (0,))
+    for i in range(2):
+        w_last[i] = weigh(i, q_buf.at[KVH - 1], k_win.at[KVH - 1], bias)
+    arrive(KVH - 1, (1,))
 
     for back in (1, 2):
         @pl.when(me + back < n)
@@ -260,14 +276,15 @@
         functools.partial(kernel, n),
         out_shape=[
             pltpu.VMEM((KVH - 1, rows, GROUP * HD), jnp.bfloat16),
+            pltpu.VMEM((KVH, WINDOW, HD), jnp.bfloat16),
+            pltpu.VMEM((2, GROUP * BLK, REACH), jnp.bfloat16),
+        ],
+        in_specs=[pl.BlockSpec(memory_space=pltpu.HBM)] * 4,
+        out_specs=[pl.BlockSpec(memory_space=pltpu.VMEM)] * 3,
+        scratch_shapes=[
             pltpu.VMEM((KVH, rows, GROUP * HD), jnp.bfloat16),
             pltpu.VMEM((KVH, WINDOW, HD), jnp.bfloat16),
-            pltpu.VMEM((KVH, WINDOW, HD), jnp.bfloat16),
             pltpu.VMEM((2, REACH, BLK), jnp.bfloat16),
-        ],
-        in_specs=[pl.BlockSpec(memory_space=pltpu.HBM)] * 4,
-        out_specs=[pl.BlockSpec(memory_space=pltpu.VMEM)] * 5,
-        scratch_shapes=[
             pltpu.SMEM(doc_flags.shape, jnp.int32),
             pltpu.VMEM((8, BLK), jnp.int32),
             pltpu.VMEM((2, 8, BLK), jnp.int32),
@@ -288,7 +305,7 @@
     return pl.pallas_call(
         last_kernel,
         out_shape=jax.ShapeDtypeStruct(queries.shape, jnp.bfloat16),
-        in_specs=[pl.BlockSpec(memory_space=pltpu.VMEM)] * 5,
+        in_specs=[pl.BlockSpec(memory_space=pltpu.VMEM)] * 3,
         out_specs=pl.BlockSpec(memory_space=pltpu.HBM),
         scratch_shapes=[pltpu.VMEM((rows, GROUP * HD), jnp.bfloat16), dma((KVH + 1,))],
         compiler_params=pltpu.CompilerParams(vmem_limit_bytes=32 * 1024 * 1024),

time: 24 us -> 23.6 us (0.983)
  Pallas kernels: 23.8 us -> 23.5 us
    pallas_call x1, Pallas kernels: 3.51 us -> 1.82 us  [per_device(): pl.pallas_call(last_kernel, out_shape=jax.ShapeDtypeStruct(queries.shape,...]
    pallas_call x1, Pallas kernels: 20.3 us -> 21.6 us  [per_device(): pl.pallas_call(functools.partial(kernel, n), out_shape=[pltpu.VMEM((KVH -...]
where the time goes in v4:
time: 23.6 us; the launch traced here: 23.5 us
  Pallas kernels  23.5 us (100%)
    pallas_call x1, Pallas kernels, per_device(): pl.pallas_call(functools.partial(kernel, n), out_shape=[pltpu.VMEM((KVH -...  21.6 us
    pallas_call x1, Pallas kernels, per_device(): pl.pallas_call(last_kernel, out_shape=jax.ShapeDtypeStruct(queries.shape,...  1.82 us

profile of v4, /device:TPU:21, one launch (start us, length us, event | category | flops | bytes accessed | tf_op | source)
XLA Modules:
  0.0 23.5 jit_solution(3678903818932165046)
XLA Ops:
  0.0 21.6 %window_attention.1 = (bf16[3,256,1024]{2,1,0:T(8,128)(2,1)S(1)}, bf16[4,896,128]{2,1,0:T(8,128)(2,1)S(1)}, bf16[2,1024,768]{2,1,0:T(8,128)(2,1)S(1)}) custom-call(bf16[256,4096]{1,0:T(8,128)(2,1)} %q_hbm.1, bf16[256,512]{1,0:T(8,128)(2,1)} %k_hbm.1, bf16[256,512]{1,0:T(8,128)(2,1)} %v_hbm.1, s32[2]{0:T(128)} %flags_hbm.1), custom_call_target="tpu_custom_call" | custom-call | tf_op jit(solution)/shard_map/window_attention/pallas_call | solution.py:275
  21.6 1.8 %last_group.1 = bf16[256,4096]{1,0:T(8,128)(2,1)} custom-call(bf16[3,256,1024]{2,1,0:T(8,128)(2,1)S(1)} %get-tuple-element.8.o_first, bf16[4,896,128]{2,1,0:T(8,128)(2,1)S(1)} %get-tuple-element.9.v_win, bf16[2,1024,768]{2,1,0:T(8,128)(2,1)S(1)} %get-tuple-element.10.w_last), custom_call_target="tpu_custom_call" | custom-call | tf_op jit(solution)/shard_map/last_group/pallas_call | solution.py:305

commit v5 on v4

--- a/solution.py
+++ b/solution.py
@@ -159,8 +159,6 @@
     for g in range(KVH):
         for copy in own_copies(g):
             copy.start()
-    for g in range(KVH):
-        q_copy(g).start()
     flag_copy.wait()
     flags_out[0:1, :] = jnp.full((1, BLK), flags_ref[0], jnp.int32)
     flags_out[1:2, :] = jnp.full((1, BLK), flags_ref[1], jnp.int32)
@@ -193,6 +191,8 @@
             def _():
                 for kv in kinds:
                     sends(g, back)[kv].start()
+        if 0 in kinds:
+            q_copy(g).start()
 
     for back in (1, 2):
         @pl.when(present[back])

time: 23.6 us -> 23.6 us (level)
  no operation moved by 1% of the time
where the time goes in v5:
time: 23.6 us; the launch traced here: 23.5 us
  Pallas kernels  23.5 us (100%)
    pallas_call x1, Pallas kernels, per_device(): pl.pallas_call(functools.partial(kernel, n), out_shape=[pltpu.VMEM((KVH -...  21.6 us
    pallas_call x1, Pallas kernels, per_device(): pl.pallas_call(last_kernel, out_shape=jax.ShapeDtypeStruct(queries.shape,...  1.82 us

profile of v5, /device:TPU:21, one launch (start us, length us, event | category | flops | bytes accessed | tf_op | source)
XLA Modules:
  0.0 23.5 jit_solution(16975718123715276237)
XLA Ops:
  0.0 21.6 %window_attention.1 = (bf16[3,256,1024]{2,1,0:T(8,128)(2,1)S(1)}, bf16[4,896,128]{2,1,0:T(8,128)(2,1)S(1)}, bf16[2,1024,768]{2,1,0:T(8,128)(2,1)S(1)}) custom-call(bf16[256,4096]{1,0:T(8,128)(2,1)} %q_hbm.1, bf16[256,512]{1,0:T(8,128)(2,1)} %k_hbm.1, bf16[256,512]{1,0:T(8,128)(2,1)} %v_hbm.1, s32[2]{0:T(128)} %flags_hbm.1), custom_call_target="tpu_custom_call" | custom-call | tf_op jit(solution)/shard_map/window_attention/pallas_call | solution.py:275
  21.6 1.8 %last_group.1 = bf16[256,4096]{1,0:T(8,128)(2,1)} custom-call(bf16[3,256,1024]{2,1,0:T(8,128)(2,1)S(1)} %get-tuple-element.8.o_first, bf16[4,896,128]{2,1,0:T(8,128)(2,1)S(1)} %get-tuple-element.9.v_win, bf16[2,1024,768]{2,1,0:T(8,128)(2,1)S(1)} %get-tuple-element.10.w_last), custom_call_target="tpu_custom_call" | custom-call | tf_op jit(solution)/shard_map/last_group/pallas_call | solution.py:305
